TPU v7x, 32 devices: a whole 2x2x4 slice. The times are simulated.
32 devices in a mesh: grp: 2 (over y), mesh: 16 (over z, x, core).
Axes of the slice: x: 2, y: 2, z: 4, core: 2. Of those that a mesh axis runs over, the one named last changes fastest.
Arguments:
- basis: bfloat16 [65536, 512], P(('grp', 'mesh')), parts along dimension 0, may hold values from -6 to 6
- blocks: bfloat16 [2, 512, 3, 128, 128], P(None, ('grp', 'mesh')), parts along dimension 1, may hold values from -0.0017089844 to 0.0017089844
- columns: int32 [2, 512, 2], P(None, ('grp', 'mesh')), parts along dimension 1, may hold values from 0 to 31
- sends: int32 [32, 16], P(('grp', 'mesh')), parts along dimension 0, may hold values from 0 to 15
Outputs:
- projected: float32 [1024, 1024], P(('grp', 'mesh')), parts along dimension 0
There are 2 independent parts, one for each index of `grp`. A program takes and returns all parts, laid end to end along the dimension named above; each array names one. Nothing has to cross between parts.
All inputs are finite; a program needn't handle non-finite values.
Results may differ from a plain program's by a relative error of at most 0.0029.
Values may be sent and summed in bfloat16 or wider, within the bound.
A program may use at most 64 MiB of HBM per device.

v0:
```python
import functools

import jax
import jax.numpy as jnp
from jax import lax
from jax.experimental import pallas as pl
from jax.experimental.pallas import tpu as pltpu
from jax.sharding import PartitionSpec as P

MESH = pl.DeviceIdType.MESH
CORES = 2
LANES = 128
AHEAD = 2
FAR = 1


def from_behind(value, axis, steps):
    count = lax.axis_size(axis)
    leading, last = (max(0, -steps), min(count, count - steps))
    return lax.ppermute(value, axis, [(source, source + steps) for source in range(leading, last)])


def plain_shards(basis, blocks, columns, sends):
    count_params, count_blocks, count_slots, block_size, _ = blocks.shape
    basis_width = basis.shape[1]
    halo_count = sends.shape[1] // 2
    own_blocks = basis.reshape(count_blocks, block_size, basis_width)
    diag_index = jnp.arange(count_blocks, dtype=jnp.int32)[:, None]
    images = []
    upward = jnp.take(own_blocks, sends[0, halo_count:], axis=0)
    downward = jnp.take(own_blocks, sends[0, :halo_count], axis=0)
    from_below = from_behind(upward, "mesh", 1)
    from_above = from_behind(downward, "mesh", -1)
    extended = jnp.concatenate([own_blocks, from_below, from_above], axis=0)
    for param in range(count_params):
        slot_index = jnp.concatenate([diag_index, columns[param]], axis=1)
        gathered = jnp.take(extended, slot_index, axis=0)
        accumulated = jnp.einsum(
            "bsik,bskj->bij", blocks[param], gathered, preferred_element_type=jnp.float32
        )
        images.append(
            accumulated.astype(jnp.bfloat16).reshape(count_blocks * block_size, basis_width)
        )
    stacked_images = jnp.concatenate(images, axis=1)
    return lax.psum_scatter(
        lax.dot_general(
            basis, stacked_images, (((0,), (0,)), ((), ())), preferred_element_type=jnp.float32
        ),
        "mesh",
        scatter_dimension=0,
        tiled=True,
    )


def chip_grid(chips):
    across = 1
    while (2 * across) ** 2 < chips and chips % (2 * across) == 0:
        across *= 2
    return chips // across, across


def kernel(n, zs, xs, width, basis, blocks, columns, sends, out, *scratch):
    chunks = basis.shape[2] // width
    own, scratch = scratch[:chunks], scratch[chunks:]
    ext, scratch = scratch[:chunks], scratch[chunks:]
    (
        stage, turned, ops, image, pair_out, pair_in, half_sum, z_out, z_in, x_sum, x_out, x_in, far_in,
        own_sem, ext_sem, ops_sem, halo_send, halo_recv,
        pair_send, pair_recv, z_send, z_recv, x_send, x_recv, far_send, far_recv,
    ) = scratch
    params, count, slots, size, _ = blocks.shape
    basis_width = basis.shape[2]
    rows = count * size
    halo = sends.shape[1] // 2
    half = basis_width // CORES
    each = basis_width // n
    chips = zs * xs
    hops = chunks - FAR

    me = lax.axis_index("mesh")
    core = lax.rem(me, CORES)
    chip = me // CORES
    x = lax.rem(chip, xs)
    z = chip // xs
    partner = me + 1 - 2 * core
    outer = me - 1 + 2 * core
    has_outer = jnp.logical_and(outer >= 0, outer < n)

    def at_z(step):
        return (lax.rem(z + step, zs) * xs + x) * CORES + core

    def at_x(step):
        return (z * xs + lax.rem(x + step, xs)) * CORES + core

    def own_copy(k):
        return pltpu.make_async_copy(
            basis.at[:, :, pl.ds(k * width, width)], own[k], own_sem.at[k]
        )

    def ext_copy(k):
        return pltpu.make_async_copy(
            basis.at[:, :, pl.ds(k * width, width)], ext[k].at[pl.ds(0, count)], ext_sem.at[k]
        )

    ops_copy = pltpu.make_async_copy(blocks, ops, ops_sem)

    def halo_copy(k, way):
        return pltpu.make_async_remote_copy(
            src_ref=stage.at[k, way],
            dst_ref=ext[k].at[pl.ds(count + way * halo, halo)],
            send_sem=halo_send.at[k, way],
            recv_sem=halo_recv.at[k, way],
            device_id={"mesh": me + 1 - 2 * way},
            device_id_type=MESH,
        )

    def pair_copy(k):
        return pltpu.make_async_remote_copy(
            src_ref=pair_out.at[k], dst_ref=pair_in.at[k],
            send_sem=pair_send.at[k], recv_sem=pair_recv.at[k],
            device_id={"mesh": partner}, device_id_type=MESH,
        )

    def z_copy(k, step):
        target = lax.rem(z + step, zs)
        return pltpu.make_async_remote_copy(
            src_ref=z_out.at[k, pl.ds(target * xs, xs)], dst_ref=z_in.at[k, step - 1],
            send_sem=z_send.at[k, step - 1], recv_sem=z_recv.at[k, step - 1],
            device_id={"mesh": at_z(step)}, device_id_type=MESH,
        )

    def x_copy(k, step):
        target = lax.rem(x + step, xs)
        return pltpu.make_async_remote_copy(
            src_ref=x_out.at[k, target], dst_ref=x_in.at[k, step - 1],
            send_sem=x_send.at[k, step - 1], recv_sem=x_recv.at[k, step - 1],
            device_id={"mesh": at_x(step)}, device_id_type=MESH,
        )

    def far_copy(k, step):
        target = lax.rem(chip + step, chips)
        at = k - hops
        return pltpu.make_async_remote_copy(
            src_ref=z_out.at[k, target], dst_ref=far_in.at[at, step - 1],
            send_sem=far_send.at[at, step - 1], recv_sem=far_recv.at[at, step - 1],
            device_id={"mesh": target * CORES + core}, device_id_type=MESH,
        )

    has = (me < n - 1, me > 0)
    gets = (me > 0, me < n - 1)

    def halo_start(k):
        for way in range(2):
            @pl.when(has[way])
            def _():
                halo_copy(k, way).start()

    for k in range(chunks):
        own_copy(k).start()
    barrier = pltpu.get_barrier_semaphore()
    peers = [partner] + [lax.rem(chip + s, chips) * CORES + core for s in range(1, chips)]
    for peer in peers:
        pl.semaphore_signal(barrier, inc=1, device_id={"mesh": peer}, device_id_type=MESH)

    @pl.when(has_outer)
    def _():
        pl.semaphore_signal(barrier, inc=1, device_id={"mesh": outer}, device_id_type=MESH)

    for k in range(chunks):
        ext_copy(k).start()
    ops_copy.start()

    for k in range(chunks):
        own_copy(k).wait()
        for way, first in ((0, halo), (1, 0)):
            for h in range(halo):
                stage[k, way, h] = own[k][sends[0, first + h]]
        if k == 0:
            pl.semaphore_wait(barrier, len(peers) + has_outer.astype(jnp.int32))

        if k < AHEAD:
            halo_start(k)

    for way in range(2):
        @pl.when(jnp.logical_not(gets[way]))
        def _():
            for k in range(chunks):
                ext[k][pl.ds(count + way * halo, halo)] = jnp.zeros(
                    (halo, size, width), jnp.bfloat16
                )

    per_chunk = width // each
    pair_rows = 2 * size
    for k in range(chunks):
        def turn(r, carry):
            start = pl.multiple_of(r * pair_rows, pair_rows)
            flipped = own[k][pl.ds(r * 2, 2)].reshape(pair_rows, width).T
            for q in range(per_chunk):
                d = k * per_chunk + q
                place = (d % CORES) * half + (d // CORES) * each
                turned[place:place + each, pl.ds(start, pair_rows)] = flipped[
                    q * each:(q + 1) * each
                ]
            return carry

        lax.fori_loop(0, count // 2, turn, 0)

    ops_copy.wait()
    for k in range(chunks):
        ext_copy(k).wait()

    def z_send_all(k):
        pair_copy(k).wait_recv()
        total = half_sum[k] + pair_in[k].reshape(chips, each, params * width).astype(jnp.float32)
        half_sum[k] = total
        z_out[k] = total.astype(jnp.bfloat16)
        if k < hops:
            for s in range(1, zs):
                z_copy(k, s).start()
        else:
            for s in range(1, chips):
                far_copy(k, s).start()

    def x_send_all(k):
        total = half_sum[k, pl.ds(z * xs, xs)]
        for s in range(1, zs):
            z_copy(k, s).wait_recv()
            total = total + z_in[k, s - 1].astype(jnp.float32)
        x_sum[k] = total
        x_out[k] = total.astype(jnp.bfloat16)
        for s in range(1, xs):
            x_copy(k, s).start()

    def finish(k):
        if k < hops:
            total = x_sum[k, x]
            for s in range(1, xs):
                x_copy(k, s).wait_recv()
                total = total + x_in[k, s - 1].astype(jnp.float32)
        else:
            total = half_sum[k, chip]
            for s in range(1, chips):
                far_copy(k, s).wait_recv()
                total = total + far_in[k - hops, s - 1].astype(jnp.float32)
        for p in range(params):
            out[:, p * basis_width + k * width:p * basis_width + (k + 1) * width] = total[
                :, p * width:(p + 1) * width
            ]

    for k in range(chunks):
        for way in range(2):
            @pl.when(gets[way])
            def _():
                halo_copy(k, way).wait_recv()

        def apply(g, carry):
            row = pl.multiple_of(g * size, size)
            diag = ext[k][g]
            for p in range(params):
                parts = [diag]
                for s in range(1, slots):
                    parts.append(ext[k][columns[p, s - 1, g]])
                left = jnp.concatenate([ops[p, g, s] for s in range(slots)], axis=1)
                made = jnp.dot(
                    left, jnp.concatenate(parts, axis=0), preferred_element_type=jnp.float32
                )
                image[pl.ds(row, size), p * width:(p + 1) * width] = made.astype(jnp.bfloat16)
            return carry

        lax.fori_loop(0, count, apply, 0, unroll=count)

        theirs = pl.multiple_of((1 - core) * half, half)
        pair_out[k] = jnp.dot(
            turned[pl.ds(theirs, half), :], image[...], preferred_element_type=jnp.float32
        ).astype(jnp.bfloat16)
        pair_copy(k).start()
        mine = pl.multiple_of(core * half, half)
        half_sum[k] = jnp.dot(
            turned[pl.ds(mine, half), :], image[...], preferred_element_type=jnp.float32
        ).reshape(chips, each, params * width)
        z_send_all(k)
        if k + AHEAD < chunks:
            halo_start(k + AHEAD)
        if 0 < k <= hops:
            x_send_all(k - 1)
    if FAR == 0:
        x_send_all(chunks - 1)
    for k in range(chunks):
        finish(k)

    for k in range(chunks):
        for way in range(2):
            @pl.when(has[way])
            def _():
                halo_copy(k, way).wait_send()
        pair_copy(k).wait_send()
        if k < hops:
            for s in range(1, zs):
                z_copy(k, s).wait_send()
            for s in range(1, xs):
                x_copy(k, s).wait_send()
        else:
            for s in range(1, chips):
                far_copy(k, s).wait_send()


def fused_shards(n, basis, blocks, columns, sends):
    params, count, slots, size, _ = blocks.shape
    rows, basis_width = basis.shape
    halo = sends.shape[1] // 2
    zs, xs = chip_grid(n // CORES)
    width = LANES
    chunks = basis_width // width
    each, half = basis_width // n, basis_width // CORES
    bf, f32 = jnp.bfloat16, jnp.float32
    wide = params * width
    dma = pltpu.SemaphoreType.DMA
    return pl.pallas_call(
        functools.partial(kernel, n, zs, xs, width),
        out_shape=jax.ShapeDtypeStruct((each, params * basis_width), f32),
        in_specs=[
            pl.BlockSpec(memory_space=pl.ANY),
            pl.BlockSpec(memory_space=pl.ANY),
            pl.BlockSpec(memory_space=pltpu.SMEM),
            pl.BlockSpec(memory_space=pltpu.SMEM),
        ],
        out_specs=pl.BlockSpec(memory_space=pltpu.VMEM),
        scratch_shapes=[pltpu.VMEM((count, size, width), bf) for _ in range(chunks)]
        + [pltpu.VMEM((count + 2 * halo, size, width), bf) for _ in range(chunks)]
        + [
            pltpu.VMEM((chunks, 2, halo, size, width), bf),
            pltpu.VMEM((basis_width, rows), bf),
            pltpu.VMEM(blocks.shape, bf),
            pltpu.VMEM((rows, wide), bf),
            pltpu.VMEM((chunks, half, wide), bf),
            pltpu.VMEM((chunks, half, wide), bf),
            pltpu.VMEM((chunks, zs * xs, each, wide), f32),
            pltpu.VMEM((chunks, zs * xs, each, wide), bf),
            pltpu.VMEM((chunks, zs, xs, each, wide), bf),
            pltpu.VMEM((chunks, xs, each, wide), f32),
            pltpu.VMEM((chunks, xs, each, wide), bf),
            pltpu.VMEM((chunks, xs, each, wide), bf),
            pltpu.VMEM((max(FAR, 1), zs * xs, each, wide), bf),
            dma((chunks,)),
            dma((chunks,)),
            dma,
            dma((chunks, 2)),
            dma((chunks, 2)),
            dma((chunks,)),
            dma((chunks,)),
            dma((chunks, zs)),
            dma((chunks, zs)),
            dma((chunks, xs)),
            dma((chunks, xs)),
            dma((max(FAR, 1), zs * xs)),
            dma((max(FAR, 1), zs * xs)),
        ],
        compiler_params=pltpu.CompilerParams(collective_id=0, has_side_effects=True),
    )(basis.reshape(count, size, basis_width), blocks, jnp.swapaxes(columns, 1, 2), sends)


def solution(mesh):
    n = mesh.shape["mesh"]

    def shards(basis, blocks, columns, sends):
        each = basis.shape[1] // n
        tiled = basis.shape[1] % (n * 16) == 0 and LANES % max(each, 1) == 0
        if n % CORES == 0 and tiled and blocks.shape[3] == LANES:
            return fused_shards(n, basis, blocks, columns, sends)
        return plain_shards(basis, blocks, columns, sends)

    placed = (
        P(("grp", "mesh"), None),
        P(None, ("grp", "mesh"), None, None, None),
        P(None, ("grp", "mesh"), None),
        P(("grp", "mesh"), None),
    )
    return jax.shard_map(
        shards, mesh=mesh, in_specs=placed, out_specs=P(("grp", "mesh"), None), check_vma=False
    )
```

profile of v0, /device:TPU:0, one launch (start us, length us, event | category | flops | bytes accessed | tf_op | source)
XLA Modules:
  0.0 41.6 jit_solution(6290890945256874882)
XLA Ops:
  0.0 40.0 %shard_map.46 = f32[32,1024]{1,0:T(8,128)} custom-call(bf16[16,128,512]{2,1,0:T(8,128)(2,1)} %bitcast.2, bf16[2,16,3,128,128]{4,3,2,1,0:T(8,128)(2,1)} %blocks.1, s32[2,2,16]{2,1,0:T(2,128)} %bitcast.3, s32[1,16]{1,0:T(1,128)} %sends.1), custom_call_target="tpu_custom_call" | custom-call | tf_op jit(solution)/shard_map/pallas_call | solution.py:318
  40.0 1.6 %copy.6 = f32[32,1024]{1,0:T(8,128)} copy(f32[32,1024]{1,0:T(8,128)} %shard_map.46) | data formatting | bytes 262144
where the time goes:
time: 41.7 us; the launch traced here: 41.6 us
  Pallas kernels  40 us (96%)
  local copies, waits for them, and re-layouts  1.57 us (4%)
    pallas_call x1, Pallas kernels, fused_shards(): pl.pallas_call(functools.partial(kernel, n, zs, xs, width), out_shape=jax...  40 us
    unnamed x1, local copies, waits for them, and re-layouts  1.57 us

commit v1 on v0

v1 whole, which is shorter than its diff:
```python
import functools

import jax
import jax.numpy as jnp
from jax import lax
from jax.experimental import pallas as pl
from jax.experimental.pallas import tpu as pltpu
from jax.sharding import PartitionSpec as P

MESH = pl.DeviceIdType.MESH
CORES = 2
LANES = 128
XS = 2
FAR = 1
SERVED = 3


def from_behind(value, axis, steps):
    count = lax.axis_size(axis)
    leading, last = (max(0, -steps), min(count, count - steps))
    return lax.ppermute(value, axis, [(source, source + steps) for source in range(leading, last)])


def plain_shards(basis, blocks, columns, sends):
    count_params, count_blocks, count_slots, block_size, _ = blocks.shape
    basis_width = basis.shape[1]
    halo_count = sends.shape[1] // 2
    own_blocks = basis.reshape(count_blocks, block_size, basis_width)
    diag_index = jnp.arange(count_blocks, dtype=jnp.int32)[:, None]
    images = []
    upward = jnp.take(own_blocks, sends[0, halo_count:], axis=0)
    downward = jnp.take(own_blocks, sends[0, :halo_count], axis=0)
    from_below = from_behind(upward, "mesh", 1)
    from_above = from_behind(downward, "mesh", -1)
    extended = jnp.concatenate([own_blocks, from_below, from_above], axis=0)
    for param in range(count_params):
        slot_index = jnp.concatenate([diag_index, columns[param]], axis=1)
        gathered = jnp.take(extended, slot_index, axis=0)
        accumulated = jnp.einsum(
            "bsik,bskj->bij", blocks[param], gathered, preferred_element_type=jnp.float32
        )
        images.append(
            accumulated.astype(jnp.bfloat16).reshape(count_blocks * block_size, basis_width)
        )
    stacked_images = jnp.concatenate(images, axis=1)
    return lax.psum_scatter(
        lax.dot_general(
            basis, stacked_images, (((0,), (0,)), ((), ())), preferred_element_type=jnp.float32
        ),
        "mesh",
        scatter_dimension=0,
        tiled=True,
    )


def kernel(n, zs, width, basis, blocks, columns, sends, out, *scratch):
    chunks = basis.shape[2] // width
    own, scratch = scratch[:chunks], scratch[chunks:]
    ext, scratch = scratch[:chunks], scratch[chunks:]
    (
        stage, relay, turned, ops, image, part, pair_out, pair_in, z_out, z_in, x_own, x_out, x_in, far_in,
        own_sem, ext_sem, ops_sem, halo_send, halo_recv, relay_recv, forward_send,
        pair_send, pair_recv, z_send, z_recv, x_send, x_recv, far_send, far_recv, rounds, go,
    ) = scratch
    params, count, slots, size, _ = blocks.shape
    basis_width = basis.shape[2]
    halo = sends.shape[1] // 2
    half = basis_width // 2
    each = basis_width // n
    chips = n // CORES
    plane = XS * CORES
    tall = plane * each
    last = chunks - 1
    hops = last - FAR

    me = lax.axis_index("mesh")
    core = lax.rem(me, CORES)
    chip = me // CORES
    x = lax.rem(chip, XS)
    z = chip // XS
    early = core == x
    late = core != x

    def at(z, x, core):
        return (z * XS + x) * CORES + core

    partner = at(z, x, 1 - core)
    mate = at(z, 1 - x, 1 - core)
    outer = me - 1 + 2 * core
    has_outer = jnp.logical_and(outer >= 0, outer < n)
    onward = z + 1 - 2 * x
    relayed = (
        relays_out(zs, chunks, z, 1) * x + relays_out(zs, chunks, z, 0) * (1 - x)
    )
    relaying = (
        relays_out(zs, chunks, z, 0) * x + relays_out(zs, chunks, z, 1) * (1 - x)
    )

    def local_copy(k, buffers, sems):
        return pltpu.make_async_copy(
            basis.at[:, :, pl.ds(k * width, width)], buffers[k].at[pl.ds(0, count)], sems.at[k]
        )

    ops_copy = pltpu.make_async_copy(blocks, ops, ops_sem)

    def remote(source, target, sent, received, device):
        return pltpu.make_async_remote_copy(
            src_ref=source, dst_ref=target, send_sem=sent, recv_sem=received,
            device_id={"mesh": device}, device_id_type=MESH,
        )

    def pair_halo(k):
        return remote(
            stage.at[k, core], ext[k].at[pl.ds(count + core * halo, halo)],
            halo_send.at[k, 0], halo_recv.at[k, 0], partner,
        )

    def outer_halo(k):
        return remote(
            stage.at[k, 1 - core], ext[k].at[pl.ds(count + (1 - core) * halo, halo)],
            halo_send.at[k, 1], halo_recv.at[k, 1], outer,
        )

    def relay_halo(k):
        return remote(
            stage.at[k, 1 - core], relay.at[k], halo_send.at[k, 1], relay_recv.at[k], mate
        )

    def forward_halo(k):
        return remote(
            relay.at[k], ext[k].at[pl.ds(count + core * halo, halo)],
            forward_send.at[k], halo_recv.at[k, 1], at(onward, x, core),
        )

    def pair_copy(k, h):
        return remote(
            pair_out.at[k, pl.ds(h * half, half)], pair_in.at[k, pl.ds(h * half, half)],
            pair_send.at[k, h], pair_recv.at[k, h], partner,
        )

    def z_copy(k, step):
        target = lax.rem(z + step, zs)
        return remote(
            z_out.at[k, pl.ds(target * tall, tall)], z_in.at[k, step - 1],
            z_send.at[k], z_recv.at[k], at(target, x, core),
        )

    def z_all(k):
        came = z_in.at[k, pl.ds(0, zs - 1)]
        return remote(came, came, z_send.at[k], z_recv.at[k], partner)

    def x_copy(k, which):
        to_x = x if which == 2 else 1 - x
        to_core = core if which == 1 else 1 - core
        slot = 0 if which == 2 else 1
        return remote(
            x_out.at[k, pl.ds((to_x * CORES + to_core) * each, each)], x_in.at[k, slot],
            x_send.at[k], x_recv.at[k, slot], at(z, to_x, to_core),
        )

    def far_copy(k, d):
        slot = lax.rem(chip - d // CORES + 2 * chips - 1, chips)
        return remote(
            z_out.at[k, pl.ds(d * each, each)], far_in.at[k - hops, slot],
            far_send.at[k - hops], far_recv.at[k - hops], d,
        )

    near = [(None, partner), (None, mate), (z > 0, at(z - 1, x, core)), (z < zs - 1, at(z + 1, x, core))]
    near_count = 2 + (z > 0).astype(jnp.int32) + (z < zs - 1).astype(jnp.int32)

    def tell(sem, peers):
        for there, peer in peers:
            if there is None:
                pl.semaphore_signal(sem, inc=1, device_id={"mesh": peer}, device_id_type=MESH)
            else:
                @pl.when(there)
                def _():
                    pl.semaphore_signal(sem, inc=1, device_id={"mesh": peer}, device_id_type=MESH)

    for k in range(chunks):
        local_copy(k, own, own_sem).start()
    barrier = pltpu.get_barrier_semaphore()
    crossing = jnp.logical_and(early, has_outer)
    tell(barrier, near + [(crossing, outer)])
    for k in range(chunks):
        local_copy(k, ext, ext_sem).start()
    ops_copy.start()

    for k in range(chunks):
        local_copy(k, own, own_sem).wait()
        for way, first in ((0, halo), (1, 0)):
            for h in range(halo):
                stage[k, way, h] = own[k][sends[0, first + h]]
        if k == 0:
            pl.semaphore_wait(barrier, near_count + crossing.astype(jnp.int32))
            tell(rounds.at[0], near)

        @pl.when(jnp.logical_and(early, k >= chunks - relayed))
        def _():
            relay_halo(k).start()

        @pl.when(jnp.logical_and(crossing, k < chunks - relayed))
        def _():
            outer_halo(k).start()

        if k == 0:
            @pl.when(late)
            def _():
                outer_halo(k).start()
        else:
            @pl.when(jnp.logical_and(late, relayed == 0))
            def _():
                outer_halo(k).start()
        pair_halo(k).start()

    @pl.when(jnp.logical_not(has_outer))
    def _():
        for k in range(chunks):
            ext[k][pl.ds(count + core * halo, halo)] = jnp.zeros((halo, size, width), jnp.bfloat16)

    pair_rows = 2 * size
    for k in range(chunks):
        def turn(r, carry):
            start = pl.multiple_of(r * pair_rows, pair_rows)
            turned[k * width:(k + 1) * width, pl.ds(start, pair_rows)] = (
                own[k][pl.ds(r * 2, 2)].reshape(pair_rows, width).T
            )
            return carry

        lax.fori_loop(0, count // 2, turn, 0)

    for r in range(zs):
        pl.semaphore_wait(rounds.at[r], near_count)
        if r + 1 < zs:
            tell(rounds.at[r + 1], near)

    ops_copy.wait()
    for k in range(chunks):
        local_copy(k, ext, ext_sem).wait()

    @pl.when(jnp.logical_and(late, relayed > 0))
    def _():
        pl.semaphore_wait(go, 1)
        for k in range(1, chunks):
            outer_halo(k).start()

    def serve(k):
        @pl.when(jnp.logical_and(early, k >= chunks - relaying))
        def _():
            relay_in(k).wait_recv()
            forward_halo(k).start()

        @pl.when(jnp.logical_and(early, k >= chunks - relayed))
        def _():
            relay_halo(k).wait_send()
            if k == last:
                pl.semaphore_signal(go, inc=1, device_id={"mesh": partner}, device_id_type=MESH)

    def relay_in(k):
        return remote(relay.at[k], relay.at[k], halo_send.at[k, 1], relay_recv.at[k], mate)

    def compute(k):
        pair_halo(k).wait_recv()

        @pl.when(has_outer)
        def _():
            forward_halo(k).wait_recv()

        def apply(g, carry):
            row = pl.multiple_of(g * size, size)
            diag = ext[k][g]
            for p in range(params):
                parts = [diag]
                for s in range(1, slots):
                    parts.append(ext[k][columns[p, s - 1, g]])
                left = jnp.concatenate([ops[p, g, s] for s in range(slots)], axis=1)
                made = jnp.dot(
                    left, jnp.concatenate(parts, axis=0), preferred_element_type=jnp.float32
                )
                image[pl.ds(row, size), p * width:(p + 1) * width] = made.astype(jnp.bfloat16)
            return carry

        lax.fori_loop(0, count, apply, 0, unroll=count)
        for h in range(2):
            made = jnp.dot(
                turned[h * half:(h + 1) * half, :], image[...], preferred_element_type=jnp.float32
            )
            part[k, h * half:(h + 1) * half] = made
            pair_out[k, h * half:(h + 1) * half] = made.astype(jnp.bfloat16)

            @pl.when(late if k < last else early)
            def _():
                pair_copy(k, h).start()

            if k == last:
                @pl.when(late)
                def _():
                    join(k, h)
                    far_start(k, range(h * n // 2, (h + 1) * n // 2))

    def join(k, h):
        pair_copy(k, h).wait_recv()
        rows = pl.ds(h * half, half)
        total = part[k, rows] + pair_in[k, rows].astype(jnp.float32)
        part[k, rows] = total
        z_out[k, rows] = total.astype(jnp.bfloat16)

    def far_start(k, devices):
        for d in devices:
            @pl.when(d != me)
            def _():
                far_copy(k, d).start()

    def gather(k):
        for h in range(2):
            join(k, h)
        if k < hops:
            for s in range(1, zs):
                z_copy(k, s).start()
        else:
            far_start(k, range(n))

    def across(k):
        total = part[k, pl.ds(pl.multiple_of(z * tall, tall), tall)]
        z_all(k).wait_recv()
        for s in range(1, zs):
            total = total + z_in[k, s - 1].astype(jnp.float32)
        x_own[k] = total
        x_out[k] = total.astype(jnp.bfloat16)
        for which in range(3):
            x_copy(k, which).start()

    def put(k, total):
        for p in range(params):
            out[:, p * basis_width + k * width:p * basis_width + (k + 1) * width] = total[
                :, p * width:(p + 1) * width
            ]

    def x_arrived(k, slot):
        remote(
            x_in.at[k, slot], x_in.at[k, slot], x_send.at[k], x_recv.at[k, slot], partner
        ).wait_recv()
        return x_in[k, slot].astype(jnp.float32)

    def finish_staged(k, mine):
        if mine:
            first = x_own[k, pl.ds(pl.multiple_of((x * CORES + core) * each, each), each)]
        else:
            first = x_arrived(k, 0)
        put(k, first + x_arrived(k, 1))

    def finish_far(k, mine):
        if mine:
            total = part[k, pl.ds(pl.multiple_of(me * each, each), each)]
        else:
            total = jnp.zeros((each, params * width), jnp.float32)
        came = chips - 1 if mine else chips
        remote(
            far_in.at[k - hops, pl.ds(0, came)], far_in.at[k - hops, pl.ds(0, came)],
            far_send.at[k - hops], far_recv.at[k - hops], partner,
        ).wait_recv()
        for s in range(came):
            total = total + far_in[k - hops, s].astype(jnp.float32)
        put(k, total)

    def finish(k, mine):
        if k < hops:
            finish_staged(k, mine)
        else:
            finish_far(k, mine)

    for k in range(min(SERVED, chunks)):
        serve(k)
    for k in range(chunks):
        if k + SERVED < chunks:
            serve(k + SERVED)
        compute(k)
        if k == last - 1:
            @pl.when(early)
            def _():
                gather(0)

    @pl.when(early)
    def _():
        for k in range(1, last):
            gather(k)
            if k - 1 < hops:
                across(k - 1)
        for k in range(last - 1, hops):
            across(k)
        for k in range(chunks):
            finish(k, k < last)

    @pl.when(late)
    def _():
        for k in range(chunks):
            finish(k, k == last)

    for k in range(chunks):
        pair_halo(k).wait_send()

        @pl.when(jnp.logical_or(late, jnp.logical_and(crossing, k < chunks - relayed)))
        def _():
            outer_halo(k).wait_send()

        @pl.when(jnp.logical_and(early, k >= chunks - relaying))
        def _():
            forward_halo(k).wait_send()

        @pl.when(late if k < last else early)
        def _():
            for h in range(2):
                pair_copy(k, h).wait_send()

        @pl.when(early if k < last else late)
        def _():
            if k < hops:
                z_all(k).wait_send()
                remote(
                    x_out.at[k, pl.ds(0, 3 * each)], x_out.at[k, pl.ds(0, 3 * each)],
                    x_send.at[k], x_recv.at[k, 0], partner,
                ).wait_send()
            else:
                rows = pl.ds(0, (n - 1) * each)
                remote(
                    z_out.at[k, rows], z_out.at[k, rows],
                    far_send.at[k - hops], far_recv.at[k - hops], partner,
                ).wait_send()


def relays_out(zs, chunks, z, x):
    if x == 1:
        return jnp.where(z < zs - 1, jnp.clip(chunks - z, 0, chunks), 0)
    return jnp.clip(z - 1, 0, chunks)


def fused_shards(n, basis, blocks, columns, sends):
    params, count, slots, size, _ = blocks.shape
    rows, basis_width = basis.shape
    halo = sends.shape[1] // 2
    zs = n // (CORES * XS)
    width = LANES
    chunks = basis_width // width
    each = basis_width // n
    tall = XS * CORES * each
    bf, f32 = jnp.bfloat16, jnp.float32
    wide = params * width
    dma = pltpu.SemaphoreType.DMA
    hops = chunks - 1 - FAR
    return pl.pallas_call(
        functools.partial(kernel, n, zs, width),
        out_shape=pltpu.VMEM((each, params * basis_width), f32),
        in_specs=[
            pl.BlockSpec(memory_space=pl.ANY),
            pl.BlockSpec(memory_space=pl.ANY),
            pl.BlockSpec(memory_space=pltpu.SMEM),
            pl.BlockSpec(memory_space=pltpu.SMEM),
        ],
        out_specs=pl.BlockSpec(memory_space=pltpu.VMEM),
        scratch_shapes=[pltpu.VMEM((count, size, width), bf) for _ in range(chunks)]
        + [pltpu.VMEM((count + 2 * halo, size, width), bf) for _ in range(chunks)]
        + [
            pltpu.VMEM((chunks, 2, halo, size, width), bf),
            pltpu.VMEM((chunks, halo, size, width), bf),
            pltpu.VMEM((basis_width, rows), bf),
            pltpu.VMEM(blocks.shape, bf),
            pltpu.VMEM((rows, wide), bf),
            pltpu.VMEM((chunks, basis_width, wide), f32),
            pltpu.VMEM((chunks, basis_width, wide), bf),
            pltpu.VMEM((chunks, basis_width, wide), bf),
            pltpu.VMEM((chunks, basis_width, wide), bf),
            pltpu.VMEM((hops, zs, tall, wide), bf),
            pltpu.VMEM((hops, tall, wide), f32),
            pltpu.VMEM((hops, tall, wide), bf),
            pltpu.VMEM((hops, 2, each, wide), bf),
            pltpu.VMEM((chunks - hops, n // CORES, each, wide), bf),
            dma((chunks,)),
            dma((chunks,)),
            dma,
            dma((chunks, 2)),
            dma((chunks, 2)),
            dma((chunks,)),
            dma((chunks,)),
            dma((chunks, 2)),
            dma((chunks, 2)),
            dma((hops,)),
            dma((hops,)),
            dma((hops,)),
            dma((hops, 2)),
            dma((chunks - hops,)),
            dma((chunks - hops,)),
            pltpu.SemaphoreType.REGULAR((zs,)),
            pltpu.SemaphoreType.REGULAR,
        ],
        compiler_params=pltpu.CompilerParams(collective_id=0, has_side_effects=True),
    )(basis.reshape(count, size, basis_width), blocks, jnp.swapaxes(columns, 1, 2), sends)


def solution(mesh):
    n = mesh.shape["mesh"]

    def shards(basis, blocks, columns, sends):
        each = basis.shape[1] // n
        tiled = basis.shape[1] % (n * 16) == 0 and LANES % max(each, 1) == 0
        chunked = basis.shape[1] // LANES > FAR + 1 and n % (XS * CORES) == 0
        if chunked and tiled and blocks.shape[3] == LANES:
            return fused_shards(n, basis, blocks, columns, sends)
        return plain_shards(basis, blocks, columns, sends)

    placed = (
        P(("grp", "mesh"), None),
        P(None, ("grp", "mesh"), None, None, None),
        P(None, ("grp", "mesh"), None),
        P(("grp", "mesh"), None),
    )
    return jax.shard_map(
        shards, mesh=mesh, in_specs=placed, out_specs=P(("grp", "mesh"), None), check_vma=False
    )
```

time: 41.7 us -> 39.2 us (0.940)
  the two profiles are of different devices: /device:TPU:0 before, /device:TPU:27 now
where the time goes in v1:
time: 39.2 us; the launch traced here: 39 us
  Pallas kernels  38.4 us (98%)
  local copies, waits for them, and re-layouts  0.66 us (2%)
    pallas_call x1, Pallas kernels, fused_shards(): pl.pallas_call(functools.partial(kernel, n, zs, width), out_shape=pltpu.V...  38.4 us

profile of v1, /device:TPU:27, one launch (start us, length us, event | category | flops | bytes accessed | tf_op | source)
XLA Modules:
  0.0 39.0 jit_solution(17798511250711231681)
XLA Ops:
  0.0 38.4 %shard_map.46 = f32[32,1024]{1,0:T(8,128)S(1)} custom-call(bf16[16,128,512]{2,1,0:T(8,128)(2,1)} %bitcast.2, bf16[2,16,3,128,128]{4,3,2,1,0:T(8,128)(2,1)} %blocks.1, s32[2,2,16]{2,1,0:T(2,128)} %bitcast.3, s32[1,16]{1,0:T(1,128)} %sends.1), custom_call_target="tpu_custom_call" | custom-call | tf_op jit(solution)/shard_map/pallas_call | solution.py:450
  38.4 0.7 %copy.6 = f32[32,1024]{1,0:T(8,128)} copy(f32[32,1024]{1,0:T(8,128)S(1)} %shard_map.46) | data formatting | bytes 262144

commit v2 on v1

--- a/solution.py
+++ b/solution.py
@@ -11,8 +11,10 @@
 CORES = 2
 LANES = 128
 XS = 2
-FAR = 1
-SERVED = 3
+FAR = 2
+SERVED = 2
+LAG = 1
+GATED = 2
 
 
 def from_behind(value, axis, steps):
@@ -71,7 +73,7 @@
     plane = XS * CORES
     tall = plane * each
     last = chunks - 1
-    hops = last - FAR
+    hops = chunks - FAR
 
     me = lax.axis_index("mesh")
     core = lax.rem(me, CORES)
@@ -208,7 +210,7 @@
             def _():
                 outer_halo(k).start()
         else:
-            @pl.when(jnp.logical_and(late, relayed == 0))
+            @pl.when(jnp.logical_and(late, relayed < GATED))
             def _():
                 outer_halo(k).start()
         pair_halo(k).start()
@@ -238,23 +240,27 @@
     for k in range(chunks):
         local_copy(k, ext, ext_sem).wait()
 
-    @pl.when(jnp.logical_and(late, relayed > 0))
+    @pl.when(jnp.logical_and(late, relayed >= GATED))
     def _():
         pl.semaphore_wait(go, 1)
         for k in range(1, chunks):
             outer_halo(k).start()
 
     def serve(k):
+        @pl.when(jnp.logical_and(early, k >= chunks - relayed))
+        def _():
+            relay_halo(k).wait_send()
+            if k == last:
+                @pl.when(relayed >= GATED)
+                def _():
+                    pl.semaphore_signal(
+                        go, inc=1, device_id={"mesh": partner}, device_id_type=MESH
+                    )
+
         @pl.when(jnp.logical_and(early, k >= chunks - relaying))
         def _():
             relay_in(k).wait_recv()
             forward_halo(k).start()
-
-        @pl.when(jnp.logical_and(early, k >= chunks - relayed))
-        def _():
-            relay_halo(k).wait_send()
-            if k == last:
-                pl.semaphore_signal(go, inc=1, device_id={"mesh": partner}, device_id_type=MESH)
 
     def relay_in(k):
         return remote(relay.at[k], relay.at[k], halo_send.at[k, 1], relay_recv.at[k], mate)
@@ -288,11 +294,11 @@
             part[k, h * half:(h + 1) * half] = made
             pair_out[k, h * half:(h + 1) * half] = made.astype(jnp.bfloat16)
 
-            @pl.when(late if k < last else early)
+            @pl.when(late if k < hops else early)
             def _():
                 pair_copy(k, h).start()
 
-            if k == last:
+            if k >= hops:
                 @pl.when(late)
                 def _():
                     join(k, h)
@@ -314,11 +320,8 @@
     def gather(k):
         for h in range(2):
             join(k, h)
-        if k < hops:
-            for s in range(1, zs):
-                z_copy(k, s).start()
-        else:
-            far_start(k, range(n))
+        for s in range(1, zs):
+            z_copy(k, s).start()
 
     def across(k):
         total = part[k, pl.ds(pl.multiple_of(z * tall, tall), tall)]
@@ -375,26 +378,24 @@
         if k + SERVED < chunks:
             serve(k + SERVED)
         compute(k)
-        if k == last - 1:
+        if 0 <= k - LAG < hops:
             @pl.when(early)
             def _():
-                gather(0)
+                gather(k - LAG)
 
     @pl.when(early)
     def _():
-        for k in range(1, last):
+        for k in range(max(chunks - LAG, 0), hops):
             gather(k)
-            if k - 1 < hops:
-                across(k - 1)
-        for k in range(last - 1, hops):
+        for k in range(hops):
             across(k)
         for k in range(chunks):
-            finish(k, k < last)
+            finish(k, k < hops)
 
     @pl.when(late)
     def _():
         for k in range(chunks):
-            finish(k, k == last)
+            finish(k, k >= hops)
 
     for k in range(chunks):
         pair_halo(k).wait_send()
@@ -407,12 +408,12 @@
         def _():
             forward_halo(k).wait_send()
 
-        @pl.when(late if k < last else early)
+        @pl.when(late if k < hops else early)
         def _():
             for h in range(2):
                 pair_copy(k, h).wait_send()
 
-        @pl.when(early if k < last else late)
+        @pl.when(early if k < hops else late)
         def _():
             if k < hops:
                 z_all(k).wait_send()
@@ -430,7 +431,7 @@
 
 def relays_out(zs, chunks, z, x):
     if x == 1:
-        return jnp.where(z < zs - 1, jnp.clip(chunks - z, 0, chunks), 0)
+        return jnp.where(z < zs - 1, jnp.clip(chunks - 1 - z, 0, chunks), 0)
     return jnp.clip(z - 1, 0, chunks)
 
 
@@ -446,7 +447,7 @@
     bf, f32 = jnp.bfloat16, jnp.float32
     wide = params * width
     dma = pltpu.SemaphoreType.DMA
-    hops = chunks - 1 - FAR
+    hops = chunks - FAR
     return pl.pallas_call(
         functools.partial(kernel, n, zs, width),
         out_shape=pltpu.VMEM((each, params * basis_width), f32),
@@ -502,7 +503,7 @@
     def shards(basis, blocks, columns, sends):
         each = basis.shape[1] // n
         tiled = basis.shape[1] % (n * 16) == 0 and LANES % max(each, 1) == 0
-        chunked = basis.shape[1] // LANES > FAR + 1 and n % (XS * CORES) == 0
+        chunked = basis.shape[1] // LANES > FAR and n % (XS * CORES) == 0
         if chunked and tiled and blocks.shape[3] == LANES:
             return fused_shards(n, basis, blocks, columns, sends)
         return plain_shards(basis, blocks, columns, sends)

time: 39.2 us -> 36.6 us (0.934)
  the two profiles are of different devices: /device:TPU:27 before, /device:TPU:0 now
where the time goes in v2:
time: 36.6 us; the launch traced here: 36.4 us
  Pallas kernels  35.7 us (98%)
  local copies, waits for them, and re-layouts  0.66 us (2%)
    pallas_call x1, Pallas kernels, fused_shards(): pl.pallas_call(functools.partial(kernel, n, zs, width), out_shape=pltpu.V...  35.7 us

profile of v2, /device:TPU:0, one launch (start us, length us, event | category | flops | bytes accessed | tf_op | source)
XLA Modules:
  0.0 36.4 jit_solution(12438240092689330381)
XLA Ops:
  0.0 35.7 %shard_map.46 = f32[32,1024]{1,0:T(8,128)S(1)} custom-call(bf16[16,128,512]{2,1,0:T(8,128)(2,1)} %bitcast.2, bf16[2,16,3,128,128]{4,3,2,1,0:T(8,128)(2,1)} %blocks.1, s32[2,2,16]{2,1,0:T(2,128)} %bitcast.3, s32[1,16]{1,0:T(1,128)} %sends.1), custom_call_target="tpu_custom_call" | custom-call | tf_op jit(solution)/shard_map/pallas_call | solution.py:451
  35.8 0.7 %copy.6 = f32[32,1024]{1,0:T(8,128)} copy(f32[32,1024]{1,0:T(8,128)S(1)} %shard_map.46) | data formatting | bytes 262144

commit v3 on v2

--- a/solution.py
+++ b/solution.py
@@ -11,9 +11,14 @@
 CORES = 2
 LANES = 128
 XS = 2
+EARLY = 1
 FAR = 2
 SERVED = 2
 LAG = 1
+SLACK = 2
+HOP = 2
+AHEAD = 3
+CLOSE = 3
 GATED = 2
 
 
@@ -60,8 +65,8 @@
     own, scratch = scratch[:chunks], scratch[chunks:]
     ext, scratch = scratch[:chunks], scratch[chunks:]
     (
-        stage, relay, turned, ops, image, part, pair_out, pair_in, z_out, z_in, x_own, x_out, x_in, far_in,
-        own_sem, ext_sem, ops_sem, halo_send, halo_recv, relay_recv, forward_send,
+        stage, relay, turned, ops, diagonal, image, part, pair_out, pair_in, z_out, z_in, x_own, x_out, x_in,
+        far_in, own_sem, ops_sem, halo_send, halo_recv, relay_recv, forward_send,
         pair_send, pair_recv, z_send, z_recv, x_send, x_recv, far_send, far_recv, rounds, go,
     ) = scratch
     params, count, slots, size, _ = blocks.shape
@@ -74,6 +79,7 @@
     tall = plane * each
     last = chunks - 1
     hops = chunks - FAR
+    steps = zs.bit_length() - 1
 
     me = lax.axis_index("mesh")
     core = lax.rem(me, CORES)
@@ -114,61 +120,112 @@
     def pair_halo(k):
         return remote(
             stage.at[k, core], ext[k].at[pl.ds(count + core * halo, halo)],
-            halo_send.at[k, 0], halo_recv.at[k, 0], partner,
+            halo_send.at[0], halo_recv.at[chunks], partner,
         )
 
     def outer_halo(k):
         return remote(
             stage.at[k, 1 - core], ext[k].at[pl.ds(count + (1 - core) * halo, halo)],
-            halo_send.at[k, 1], halo_recv.at[k, 1], outer,
+            halo_send.at[1], halo_recv.at[k], outer,
         )
 
     def relay_halo(k):
         return remote(
-            stage.at[k, 1 - core], relay.at[k], halo_send.at[k, 1], relay_recv.at[k], mate
+            stage.at[k, 1 - core], relay.at[k], halo_send.at[2], relay_recv.at[k], mate
         )
 
     def forward_halo(k):
         return remote(
             relay.at[k], ext[k].at[pl.ds(count + core * halo, halo)],
-            forward_send.at[k], halo_recv.at[k, 1], at(onward, x, core),
-        )
-
-    def pair_copy(k, h):
-        return remote(
-            pair_out.at[k, pl.ds(h * half, half)], pair_in.at[k, pl.ds(h * half, half)],
-            pair_send.at[k, h], pair_recv.at[k, h], partner,
-        )
-
-    def z_copy(k, step):
-        target = lax.rem(z + step, zs)
-        return remote(
-            z_out.at[k, pl.ds(target * tall, tall)], z_in.at[k, step - 1],
-            z_send.at[k], z_recv.at[k], at(target, x, core),
-        )
+            forward_send, halo_recv.at[k], at(onward, x, core),
+        )
+
+    def half_rows(i):
+        return pl.ds(i * half, half)
+
+    def pair_copy(k):
+        return remote(pair_out.at[k], pair_in.at[k], pair_send, pair_recv.at[k], partner)
+
+    def blocks_sent(count, sent):
+        moved = stage.at[pl.ds(0, count), 0]
+        return remote(moved, moved, sent, halo_recv.at[0], partner)
+
+    def turn_of(k):
+        return k if k < EARLY else k - EARLY
+
+    def halving(k, b):
+        stride = 2 ** b
+        low, bit = lax.rem(z, stride), lax.rem(z // stride, 2)
+        kept = [low + bit * stride + j * 2 * stride for j in range(zs // (2 * stride))]
+        given = [low + (1 - bit) * stride + j * 2 * stride for j in range(zs // (2 * stride))]
+        return kept, given, z + (1 - 2 * bit) * stride, zs - zs // stride
+
+    def tall_rows(t):
+        return pl.ds(pl.multiple_of(t * tall, tall), tall)
+
+    def halve_start(k, b):
+        _, given, there, slot = halving(k, b)
+        for j, t in enumerate(given):
+            remote(
+                z_out.at[k, tall_rows(t)], z_in.at[k, slot + j],
+                z_send.at[turn_of(k)], z_recv.at[turn_of(k), b], at(there, x, core),
+            ).start()
+
+    def halve_add(k, b):
+        kept, _, _, slot = halving(k, b)
+        came = z_in.at[k, pl.ds(slot, len(kept))]
+        remote(came, came, z_send.at[turn_of(k)], z_recv.at[turn_of(k), b], partner).wait_recv()
+        for j, t in enumerate(kept):
+            total = part[k, tall_rows(t)] + z_in[k, slot + j].astype(jnp.float32)
+            part[k, tall_rows(t)] = total
+            z_out[k, tall_rows(t)] = total.astype(jnp.bfloat16)
+
+    def z_start(k, j):
+        target = j
+        slot = lax.rem(z - target + 2 * zs - 1, zs)
+
+        @pl.when(target != z)
+        def _():
+            remote(
+                z_out.at[k, pl.ds(target * tall, tall)], z_in.at[k, slot],
+                z_send.at[turn_of(k)], z_recv.at[turn_of(k), 0], at(target, x, core),
+            ).start()
 
     def z_all(k):
         came = z_in.at[k, pl.ds(0, zs - 1)]
-        return remote(came, came, z_send.at[k], z_recv.at[k], partner)
+        return remote(came, came, z_send.at[turn_of(k)], z_recv.at[turn_of(k), 0], partner)
 
     def x_copy(k, which):
         to_x = x if which == 2 else 1 - x
         to_core = core if which == 1 else 1 - core
         slot = 0 if which == 2 else 1
         return remote(
-            x_out.at[k, pl.ds((to_x * CORES + to_core) * each, each)], x_in.at[k, slot],
-            x_send.at[k], x_recv.at[k, slot], at(z, to_x, to_core),
-        )
-
-    def far_copy(k, d):
-        slot = lax.rem(chip - d // CORES + 2 * chips - 1, chips)
-        return remote(
-            z_out.at[k, pl.ds(d * each, each)], far_in.at[k - hops, slot],
-            far_send.at[k - hops], far_recv.at[k - hops], d,
-        )
+            x_out.at[k, pl.ds(pl.multiple_of((to_x * CORES + to_core) * each, each), each)], x_in.at[k, slot],
+            x_send.at[turn_of(k)], x_recv.at[k], at(z, to_x, to_core),
+        )
+
+    def far_start(k, i):
+        for j in range(zs // 2):
+            to_z = i * (zs // 2) + j
+            for to_x in range(XS):
+                slot = lax.rem(chip - to_z * XS - to_x + 2 * chips - 1, chips)
+                for to_core in range(CORES):
+                    owner = at(to_z, to_x, to_core)
+
+                    @pl.when(owner != me)
+                    def _():
+                        remote(
+                            z_out.at[k, pl.ds(owner * each, each)],
+                            far_in.at[k - hops, slot], far_send,
+                            far_recv.at[k - hops], owner,
+                        ).start()
 
     near = [(None, partner), (None, mate), (z > 0, at(z - 1, x, core)), (z < zs - 1, at(z + 1, x, core))]
     near_count = 2 + (z > 0).astype(jnp.int32) + (z < zs - 1).astype(jnp.int32)
+
+    crossing = jnp.logical_and(early, has_outer)
+    close = near[:2] + [(crossing, outer)]
+    close_count = 2 + crossing.astype(jnp.int32)
 
     def tell(sem, peers):
         for there, peer in peers:
@@ -182,26 +239,24 @@
     for k in range(chunks):
         local_copy(k, own, own_sem).start()
     barrier = pltpu.get_barrier_semaphore()
-    crossing = jnp.logical_and(early, has_outer)
-    tell(barrier, near + [(crossing, outer)])
-    for k in range(chunks):
-        local_copy(k, ext, ext_sem).start()
+    tell(barrier, close)
     ops_copy.start()
 
     for k in range(chunks):
         local_copy(k, own, own_sem).wait()
+        local_copy(k, ext, own_sem).start()
         for way, first in ((0, halo), (1, 0)):
             for h in range(halo):
                 stage[k, way, h] = own[k][sends[0, first + h]]
         if k == 0:
-            pl.semaphore_wait(barrier, near_count + crossing.astype(jnp.int32))
-            tell(rounds.at[0], near)
+            pl.semaphore_wait(barrier, close_count)
+            tell(rounds.at[0], close)
 
         @pl.when(jnp.logical_and(early, k >= chunks - relayed))
         def _():
             relay_halo(k).start()
 
-        @pl.when(jnp.logical_and(crossing, k < chunks - relayed))
+        @pl.when(jnp.logical_and(crossing, k < jnp.minimum(chunks - relayed, AHEAD)))
         def _():
             outer_halo(k).start()
 
@@ -231,14 +286,24 @@
 
         lax.fori_loop(0, count // 2, turn, 0)
 
-    for r in range(zs):
-        pl.semaphore_wait(rounds.at[r], near_count)
-        if r + 1 < zs:
-            tell(rounds.at[r + 1], near)
+    for r in range(zs + 1):
+        pl.semaphore_wait(rounds.at[r], close_count if r < CLOSE else near_count)
+        if r < zs:
+            tell(rounds.at[r + 1], close if r + 1 < CLOSE else near)
 
     ops_copy.wait()
     for k in range(chunks):
-        local_copy(k, ext, ext_sem).wait()
+        local_copy(k, ext, own_sem).wait()
+
+    def precompute(g, carry):
+        row = pl.multiple_of(g * size, size)
+        for p in range(params):
+            diagonal[pl.ds(row, size), p * width:(p + 1) * width] = jnp.dot(
+                ops[p, g, 0], own[last][g], preferred_element_type=jnp.float32
+            )
+        return carry
+
+    lax.fori_loop(0, count, precompute, 0, unroll=2)
 
     @pl.when(jnp.logical_and(late, relayed >= GATED))
     def _():
@@ -247,15 +312,15 @@
             outer_halo(k).start()
 
     def serve(k):
-        @pl.when(jnp.logical_and(early, k >= chunks - relayed))
-        def _():
-            relay_halo(k).wait_send()
-            if k == last:
-                @pl.when(relayed >= GATED)
+        if k == last:
+            for c in range(1, chunks + 1):
+                @pl.when(jnp.logical_and(early, relayed == c))
                 def _():
-                    pl.semaphore_signal(
-                        go, inc=1, device_id={"mesh": partner}, device_id_type=MESH
-                    )
+                    blocks_sent(c, halo_send.at[2]).wait_send()
+                    if c >= GATED:
+                        pl.semaphore_signal(
+                            go, inc=1, device_id={"mesh": partner}, device_id_type=MESH
+                        )
 
         @pl.when(jnp.logical_and(early, k >= chunks - relaying))
         def _():
@@ -263,10 +328,12 @@
             forward_halo(k).start()
 
     def relay_in(k):
-        return remote(relay.at[k], relay.at[k], halo_send.at[k, 1], relay_recv.at[k], mate)
+        return remote(relay.at[k], relay.at[k], halo_send.at[2], relay_recv.at[k], mate)
 
     def compute(k):
-        pair_halo(k).wait_recv()
+        if k == 0:
+            both = stage.at[:, core]
+            remote(both, both, halo_send.at[0], halo_recv.at[chunks], partner).wait_recv()
 
         @pl.when(has_outer)
         def _():
@@ -274,60 +341,78 @@
 
         def apply(g, carry):
             row = pl.multiple_of(g * size, size)
-            diag = ext[k][g]
+            first = 1 if k == last else 0
+            diag = [] if k == last else [ext[k][g]]
             for p in range(params):
-                parts = [diag]
+                parts = list(diag)
                 for s in range(1, slots):
                     parts.append(ext[k][columns[p, s - 1, g]])
-                left = jnp.concatenate([ops[p, g, s] for s in range(slots)], axis=1)
+                left = jnp.concatenate([ops[p, g, s] for s in range(first, slots)], axis=1)
                 made = jnp.dot(
                     left, jnp.concatenate(parts, axis=0), preferred_element_type=jnp.float32
                 )
+                if k == last:
+                    made = made + diagonal[pl.ds(row, size), p * width:(p + 1) * width]
                 image[pl.ds(row, size), p * width:(p + 1) * width] = made.astype(jnp.bfloat16)
             return carry
 
         lax.fori_loop(0, count, apply, 0, unroll=count)
-        for h in range(2):
+        for i in range(2):
             made = jnp.dot(
-                turned[h * half:(h + 1) * half, :], image[...], preferred_element_type=jnp.float32
+                turned[half_rows(i), :], image[...], preferred_element_type=jnp.float32
             )
-            part[k, h * half:(h + 1) * half] = made
-            pair_out[k, h * half:(h + 1) * half] = made.astype(jnp.bfloat16)
-
-            @pl.when(late if k < hops else early)
-            def _():
-                pair_copy(k, h).start()
-
-            if k >= hops:
+            part[k, half_rows(i)] = made
+            pair_out[k, half_rows(i)] = made.astype(jnp.bfloat16)
+
+            if i == 1:
+                @pl.when(late if k < EARLY else early)
+                def _():
+                    pair_copy(k).start()
+
+            if k >= EARLY:
                 @pl.when(late)
                 def _():
-                    join(k, h)
-                    far_start(k, range(h * n // 2, (h + 1) * n // 2))
-
-    def join(k, h):
-        pair_copy(k, h).wait_recv()
-        rows = pl.ds(h * half, half)
+                    join(k, i)
+                    if k < hops:
+                        z_start_half(k, i)
+                    else:
+                        far_start(k, i)
+
+    def join(k, i):
+        if i == 0:
+            pair_copy(k).wait_recv()
+        rows = half_rows(i)
         total = part[k, rows] + pair_in[k, rows].astype(jnp.float32)
         part[k, rows] = total
         z_out[k, rows] = total.astype(jnp.bfloat16)
 
-    def far_start(k, devices):
-        for d in devices:
-            @pl.when(d != me)
-            def _():
-                far_copy(k, d).start()
+    def z_start_half(k, i):
+        if i == 0:
+            for j in range(zs // 2):
+                z_start(k, j)
+        else:
+            for j in range(zs // 2, zs):
+                z_start(k, j)
 
     def gather(k):
-        for h in range(2):
-            join(k, h)
-        for s in range(1, zs):
-            z_copy(k, s).start()
+        for i in range(2):
+            join(k, i)
+        halve_start(k, 0)
+
+    def hop(k):
+        for b in range(1, steps):
+            halve_add(k, b - 1)
+            halve_start(k, b)
 
     def across(k):
-        total = part[k, pl.ds(pl.multiple_of(z * tall, tall), tall)]
-        z_all(k).wait_recv()
-        for s in range(1, zs):
-            total = total + z_in[k, s - 1].astype(jnp.float32)
+        if k < EARLY:
+            halve_add(k, steps - 1)
+            total = part[k, tall_rows(z)]
+        else:
+            total = part[k, tall_rows(z)]
+            z_all(k).wait_recv()
+            for s in range(1, zs):
+                total = total + z_in[k, s - 1].astype(jnp.float32)
         x_own[k] = total
         x_out[k] = total.astype(jnp.bfloat16)
         for which in range(3):
@@ -339,18 +424,14 @@
                 :, p * width:(p + 1) * width
             ]
 
-    def x_arrived(k, slot):
-        remote(
-            x_in.at[k, slot], x_in.at[k, slot], x_send.at[k], x_recv.at[k, slot], partner
-        ).wait_recv()
-        return x_in[k, slot].astype(jnp.float32)
-
     def finish_staged(k, mine):
+        came = x_in.at[k, pl.ds(1 if mine else 0, 1 if mine else 2)]
+        remote(came, came, x_send.at[0], x_recv.at[k], partner).wait_recv()
         if mine:
             first = x_own[k, pl.ds(pl.multiple_of((x * CORES + core) * each, each), each)]
         else:
-            first = x_arrived(k, 0)
-        put(k, first + x_arrived(k, 1))
+            first = x_in[k, 0].astype(jnp.float32)
+        put(k, first + x_in[k, 1].astype(jnp.float32))
 
     def finish_far(k, mine):
         if mine:
@@ -360,7 +441,7 @@
         came = chips - 1 if mine else chips
         remote(
             far_in.at[k - hops, pl.ds(0, came)], far_in.at[k - hops, pl.ds(0, came)],
-            far_send.at[k - hops], far_recv.at[k - hops], partner,
+            far_send, far_recv.at[k - hops], partner,
         ).wait_recv()
         for s in range(came):
             total = total + far_in[k - hops, s].astype(jnp.float32)
@@ -378,55 +459,72 @@
         if k + SERVED < chunks:
             serve(k + SERVED)
         compute(k)
-        if 0 <= k - LAG < hops:
+        if k + AHEAD < chunks:
+            @pl.when(jnp.logical_and(crossing, k + AHEAD < chunks - relayed))
+            def _():
+                outer_halo(k + AHEAD).start()
+        if 0 <= k - LAG < EARLY:
             @pl.when(early)
             def _():
                 gather(k - LAG)
+        if 0 <= k - HOP < EARLY:
+            @pl.when(early)
+            def _():
+                hop(k - HOP)
+        if EARLY <= k - SLACK < hops:
+            @pl.when(late)
+            def _():
+                across(k - SLACK)
 
     @pl.when(early)
     def _():
-        for k in range(max(chunks - LAG, 0), hops):
-            gather(k)
-        for k in range(hops):
+        for k in range(EARLY):
             across(k)
         for k in range(chunks):
-            finish(k, k < hops)
+            finish(k, k < EARLY)
 
     @pl.when(late)
     def _():
         for k in range(chunks):
-            finish(k, k >= hops)
-
-    for k in range(chunks):
-        pair_halo(k).wait_send()
-
-        @pl.when(jnp.logical_or(late, jnp.logical_and(crossing, k < chunks - relayed)))
+            finish(k, k >= EARLY)
+
+    blocks_sent(chunks, halo_send.at[0]).wait_send()
+
+    @pl.when(late)
+    def _():
+        blocks_sent(chunks, halo_send.at[1]).wait_send()
+
+    for c in range(1, chunks + 1):
+        @pl.when(jnp.logical_and(crossing, relayed == chunks - c))
         def _():
-            outer_halo(k).wait_send()
-
-        @pl.when(jnp.logical_and(early, k >= chunks - relaying))
+            blocks_sent(c, halo_send.at[1]).wait_send()
+
+        @pl.when(jnp.logical_and(early, relaying == c))
         def _():
-            forward_halo(k).wait_send()
-
-        @pl.when(late if k < hops else early)
-        def _():
-            for h in range(2):
-                pair_copy(k, h).wait_send()
-
-        @pl.when(early if k < hops else late)
-        def _():
-            if k < hops:
-                z_all(k).wait_send()
-                remote(
-                    x_out.at[k, pl.ds(0, 3 * each)], x_out.at[k, pl.ds(0, 3 * each)],
-                    x_send.at[k], x_recv.at[k, 0], partner,
-                ).wait_send()
-            else:
-                rows = pl.ds(0, (n - 1) * each)
-                remote(
-                    z_out.at[k, rows], z_out.at[k, rows],
-                    far_send.at[k - hops], far_recv.at[k - hops], partner,
-                ).wait_send()
+            blocks_sent(c, forward_send).wait_send()
+
+    def sums_sent(first, end):
+        summed = pair_out.at[pl.ds(first, end - first)]
+        remote(summed, summed, pair_send, pair_recv.at[0], partner).wait_send()
+
+    def staged_sent(k):
+        z_all(k).wait_send()
+        rows = x_out.at[k, pl.ds(0, 3 * each)]
+        remote(rows, rows, x_send.at[turn_of(k)], x_recv.at[k], partner).wait_send()
+
+    @pl.when(early)
+    def _():
+        sums_sent(EARLY, chunks)
+        for k in range(EARLY):
+            staged_sent(k)
+
+    @pl.when(late)
+    def _():
+        sums_sent(0, EARLY)
+        for k in range(EARLY, hops):
+            staged_sent(k)
+        rows = z_out.at[pl.ds(hops, chunks - hops), pl.ds(0, (n - 1) * each)]
+        remote(rows, rows, far_send, far_recv.at[0], partner).wait_send()
 
 
 def relays_out(zs, chunks, z, x):
@@ -448,6 +546,7 @@
     wide = params * width
     dma = pltpu.SemaphoreType.DMA
     hops = chunks - FAR
+    turns = max(EARLY, hops - EARLY)
     return pl.pallas_call(
         functools.partial(kernel, n, zs, width),
         out_shape=pltpu.VMEM((each, params * basis_width), f32),
@@ -465,6 +564,7 @@
             pltpu.VMEM((chunks, halo, size, width), bf),
             pltpu.VMEM((basis_width, rows), bf),
             pltpu.VMEM(blocks.shape, bf),
+            pltpu.VMEM((rows, wide), f32),
             pltpu.VMEM((rows, wide), bf),
             pltpu.VMEM((chunks, basis_width, wide), f32),
             pltpu.VMEM((chunks, basis_width, wide), bf),
@@ -476,21 +576,20 @@
             pltpu.VMEM((hops, 2, each, wide), bf),
             pltpu.VMEM((chunks - hops, n // CORES, each, wide), bf),
             dma((chunks,)),
+            dma,
+            dma((3,)),
+            dma((chunks + 1,)),
             dma((chunks,)),
             dma,
-            dma((chunks, 2)),
-            dma((chunks, 2)),
+            dma,
             dma((chunks,)),
-            dma((chunks,)),
-            dma((chunks, 2)),
-            dma((chunks, 2)),
+            dma((turns,)),
+            dma((turns, zs.bit_length() - 1)),
+            dma((turns,)),
             dma((hops,)),
-            dma((hops,)),
-            dma((hops,)),
-            dma((hops, 2)),
+            dma,
             dma((chunks - hops,)),
-            dma((chunks - hops,)),
-            pltpu.SemaphoreType.REGULAR((zs,)),
+            pltpu.SemaphoreType.REGULAR((zs + 1,)),
             pltpu.SemaphoreType.REGULAR,
         ],
         compiler_params=pltpu.CompilerParams(collective_id=0, has_side_effects=True),
@@ -503,7 +602,7 @@
     def shards(basis, blocks, columns, sends):
         each = basis.shape[1] // n
         tiled = basis.shape[1] % (n * 16) == 0 and LANES % max(each, 1) == 0
-        chunked = basis.shape[1] // LANES > FAR and n % (XS * CORES) == 0
+        chunked = basis.shape[1] // LANES >= EARLY + FAR and n // (XS * CORES) in (2, 4, 8)
         if chunked and tiled and blocks.shape[3] == LANES:
             return fused_shards(n, basis, blocks, columns, sends)
         return plain_shards(basis, blocks, columns, sends)

time: 36.6 us -> 36.3 us (level)
  no operation moved by 1% of the time
where the time goes in v3:
time: 36.3 us; the launch traced here: 36.1 us
  Pallas kernels  35.4 us (98%)
  local copies, waits for them, and re-layouts  0.66 us (2%)
    pallas_call x1, Pallas kernels, fused_shards(): pl.pallas_call(functools.partial(kernel, n, zs, width), out_shape=pltpu.V...  35.4 us

profile of v3, /device:TPU:0, one launch (start us, length us, event | category | flops | bytes accessed | tf_op | source)
XLA Modules:
  0.0 36.1 jit_solution(3612360826384065386)
XLA Ops:
  0.0 35.4 %shard_map.46 = f32[32,1024]{1,0:T(8,128)S(1)} custom-call(bf16[16,128,512]{2,1,0:T(8,128)(2,1)} %bitcast.2, bf16[2,16,3,128,128]{4,3,2,1,0:T(8,128)(2,1)} %blocks.1, s32[2,2,16]{2,1,0:T(2,128)} %bitcast.3, s32[1,16]{1,0:T(1,128)} %sends.1), custom_call_target="tpu_custom_call" | custom-call | tf_op jit(solution)/shard_map/pallas_call | solution.py:550
  35.4 0.7 %copy.6 = f32[32,1024]{1,0:T(8,128)} copy(f32[32,1024]{1,0:T(8,128)S(1)} %shard_map.46) | data formatting | bytes 262144

commit v4 on v3

--- a/solution.py
+++ b/solution.py
@@ -14,10 +14,9 @@
 EARLY = 1
 FAR = 2
 SERVED = 2
-LAG = 1
+LAG = 0
+DIRECT = ((), (0,), (1, 2, 3))
 SLACK = 2
-HOP = 2
-AHEAD = 3
 CLOSE = 3
 GATED = 2
 
@@ -79,7 +78,6 @@
     tall = plane * each
     last = chunks - 1
     hops = chunks - FAR
-    steps = zs.bit_length() - 1
 
     me = lax.axis_index("mesh")
     core = lax.rem(me, CORES)
@@ -143,8 +141,12 @@
     def half_rows(i):
         return pl.ds(i * half, half)
 
-    def pair_copy(k):
-        return remote(pair_out.at[k], pair_in.at[k], pair_send, pair_recv.at[k], partner)
+    def pair_copy(k, i):
+        rows = half_rows(i) if k == last else pl.ds(0, 2 * half)
+        return remote(
+            pair_out.at[k, rows], pair_in.at[k, rows], pair_send,
+            pair_recv.at[k + i if k == last else k], partner,
+        )
 
     def blocks_sent(count, sent):
         moved = stage.at[pl.ds(0, count), 0]
@@ -153,33 +155,6 @@
     def turn_of(k):
         return k if k < EARLY else k - EARLY
 
-    def halving(k, b):
-        stride = 2 ** b
-        low, bit = lax.rem(z, stride), lax.rem(z // stride, 2)
-        kept = [low + bit * stride + j * 2 * stride for j in range(zs // (2 * stride))]
-        given = [low + (1 - bit) * stride + j * 2 * stride for j in range(zs // (2 * stride))]
-        return kept, given, z + (1 - 2 * bit) * stride, zs - zs // stride
-
-    def tall_rows(t):
-        return pl.ds(pl.multiple_of(t * tall, tall), tall)
-
-    def halve_start(k, b):
-        _, given, there, slot = halving(k, b)
-        for j, t in enumerate(given):
-            remote(
-                z_out.at[k, tall_rows(t)], z_in.at[k, slot + j],
-                z_send.at[turn_of(k)], z_recv.at[turn_of(k), b], at(there, x, core),
-            ).start()
-
-    def halve_add(k, b):
-        kept, _, _, slot = halving(k, b)
-        came = z_in.at[k, pl.ds(slot, len(kept))]
-        remote(came, came, z_send.at[turn_of(k)], z_recv.at[turn_of(k), b], partner).wait_recv()
-        for j, t in enumerate(kept):
-            total = part[k, tall_rows(t)] + z_in[k, slot + j].astype(jnp.float32)
-            part[k, tall_rows(t)] = total
-            z_out[k, tall_rows(t)] = total.astype(jnp.bfloat16)
-
     def z_start(k, j):
         target = j
         slot = lax.rem(z - target + 2 * zs - 1, zs)
@@ -188,12 +163,12 @@
         def _():
             remote(
                 z_out.at[k, pl.ds(target * tall, tall)], z_in.at[k, slot],
-                z_send.at[turn_of(k)], z_recv.at[turn_of(k), 0], at(target, x, core),
+                z_send.at[turn_of(k)], z_recv.at[turn_of(k)], at(target, x, core),
             ).start()
 
     def z_all(k):
         came = z_in.at[k, pl.ds(0, zs - 1)]
-        return remote(came, came, z_send.at[turn_of(k)], z_recv.at[turn_of(k), 0], partner)
+        return remote(came, came, z_send.at[turn_of(k)], z_recv.at[turn_of(k)], partner)
 
     def x_copy(k, which):
         to_x = x if which == 2 else 1 - x
@@ -241,6 +216,11 @@
     barrier = pltpu.get_barrier_semaphore()
     tell(barrier, close)
     ops_copy.start()
+
+    def direct_start(k, here=True):
+        @pl.when(jnp.logical_and(jnp.logical_and(crossing, k < chunks - relayed), here))
+        def _():
+            outer_halo(k).start()
 
     for k in range(chunks):
         local_copy(k, own, own_sem).wait()
@@ -256,9 +236,8 @@
         def _():
             relay_halo(k).start()
 
-        @pl.when(jnp.logical_and(crossing, k < jnp.minimum(chunks - relayed, AHEAD)))
-        def _():
-            outer_halo(k).start()
+        if k in DIRECT[0]:
+            direct_start(k)
 
         if k == 0:
             @pl.when(late)
@@ -286,6 +265,11 @@
 
         lax.fori_loop(0, count // 2, turn, 0)
 
+    for k in DIRECT[1]:
+        direct_start(k)
+    for k in DIRECT[2][:3]:
+        direct_start(k, relayed == 0)
+
     for r in range(zs + 1):
         pl.semaphore_wait(rounds.at[r], close_count if r < CLOSE else near_count)
         if r < zs:
@@ -305,11 +289,8 @@
 
     lax.fori_loop(0, count, precompute, 0, unroll=2)
 
-    @pl.when(jnp.logical_and(late, relayed >= GATED))
-    def _():
-        pl.semaphore_wait(go, 1)
-        for k in range(1, chunks):
-            outer_halo(k).start()
+    for i, k in enumerate(DIRECT[2]):
+        direct_start(k, relayed > 0 if i < 3 else True)
 
     def serve(k):
         if k == last:
@@ -364,10 +345,10 @@
             part[k, half_rows(i)] = made
             pair_out[k, half_rows(i)] = made.astype(jnp.bfloat16)
 
-            if i == 1:
+            if i == 1 or k == last:
                 @pl.when(late if k < EARLY else early)
                 def _():
-                    pair_copy(k).start()
+                    pair_copy(k, i).start()
 
             if k >= EARLY:
                 @pl.when(late)
@@ -379,8 +360,8 @@
                         far_start(k, i)
 
     def join(k, i):
-        if i == 0:
-            pair_copy(k).wait_recv()
+        if i == 0 or k == last:
+            pair_copy(k, i).wait_recv()
         rows = half_rows(i)
         total = part[k, rows] + pair_in[k, rows].astype(jnp.float32)
         part[k, rows] = total
@@ -397,22 +378,14 @@
     def gather(k):
         for i in range(2):
             join(k, i)
-        halve_start(k, 0)
-
-    def hop(k):
-        for b in range(1, steps):
-            halve_add(k, b - 1)
-            halve_start(k, b)
+        for j in range(zs):
+            z_start(k, j)
 
     def across(k):
-        if k < EARLY:
-            halve_add(k, steps - 1)
-            total = part[k, tall_rows(z)]
-        else:
-            total = part[k, tall_rows(z)]
-            z_all(k).wait_recv()
-            for s in range(1, zs):
-                total = total + z_in[k, s - 1].astype(jnp.float32)
+        total = part[k, pl.ds(pl.multiple_of(z * tall, tall), tall)]
+        z_all(k).wait_recv()
+        for s in range(1, zs):
+            total = total + z_in[k, s - 1].astype(jnp.float32)
         x_own[k] = total
         x_out[k] = total.astype(jnp.bfloat16)
         for which in range(3):
@@ -453,24 +426,28 @@
         else:
             finish_far(k, mine)
 
-    for k in range(min(SERVED, chunks)):
+    def ungate():
+        @pl.when(jnp.logical_and(late, relayed >= GATED))
+        def _():
+            pl.semaphore_wait(go, 1)
+            for k in range(1, chunks):
+                outer_halo(k).start()
+
+    for k in range(min(SERVED + 1, chunks)):
         serve(k)
     for k in range(chunks):
-        if k + SERVED < chunks:
-            serve(k + SERVED)
         compute(k)
-        if k + AHEAD < chunks:
-            @pl.when(jnp.logical_and(crossing, k + AHEAD < chunks - relayed))
-            def _():
-                outer_halo(k + AHEAD).start()
+        if k + SERVED + 1 < chunks:
+            serve(k + SERVED + 1)
+        if k == 0:
+            ungate()
+        if k + 3 < len(DIRECT):
+            for later in DIRECT[k + 3]:
+                direct_start(later)
         if 0 <= k - LAG < EARLY:
             @pl.when(early)
             def _():
                 gather(k - LAG)
-        if 0 <= k - HOP < EARLY:
-            @pl.when(early)
-            def _():
-                hop(k - HOP)
         if EARLY <= k - SLACK < hops:
             @pl.when(late)
             def _():
@@ -582,9 +559,9 @@
             dma((chunks,)),
             dma,
             dma,
-            dma((chunks,)),
+            dma((chunks + 1,)),
             dma((turns,)),
-            dma((turns, zs.bit_length() - 1)),
+            dma((turns,)),
             dma((turns,)),
             dma((hops,)),
             dma,
@@ -602,7 +579,7 @@
     def shards(basis, blocks, columns, sends):
         each = basis.shape[1] // n
         tiled = basis.shape[1] % (n * 16) == 0 and LANES % max(each, 1) == 0
-        chunked = basis.shape[1] // LANES >= EARLY + FAR and n // (XS * CORES) in (2, 4, 8)
+        chunked = basis.shape[1] // LANES >= EARLY + FAR and n % (2 * XS * CORES) == 0
         if chunked and tiled and blocks.shape[3] == LANES:
             return fused_shards(n, basis, blocks, columns, sends)
         return plain_shards(basis, blocks, columns, sends)

time: 36.3 us -> 35.1 us (0.967)
  Pallas kernels: 35.4 us -> 34.3 us
    pallas_call x1, Pallas kernels: 35.4 us -> 34.3 us  [fused_shards(): pl.pallas_call(functools.partial(kernel, n, zs, width), out_shape=pltpu.V...]
where the time goes in v4:
time: 35.1 us; the launch traced here: 35 us
  Pallas kernels  34.3 us (98%)
  local copies, waits for them, and re-layouts  0.66 us (2%)
    pallas_call x1, Pallas kernels, fused_shards(): pl.pallas_call(functools.partial(kernel, n, zs, width), out_shape=pltpu.V...  34.3 us

profile of v4, /device:TPU:0, one launch (start us, length us, event | category | flops | bytes accessed | tf_op | source)
XLA Modules:
  0.0 35.0 jit_solution(1266628663353388104)
XLA Ops:
  0.0 34.3 %shard_map.46 = f32[32,1024]{1,0:T(8,128)S(1)} custom-call(bf16[16,128,512]{2,1,0:T(8,128)(2,1)} %bitcast.2, bf16[2,16,3,128,128]{4,3,2,1,0:T(8,128)(2,1)} %blocks.1, s32[2,2,16]{2,1,0:T(2,128)} %bitcast.3, s32[1,16]{1,0:T(1,128)} %sends.1), custom_call_target="tpu_custom_call" | custom-call | tf_op jit(solution)/shard_map/pallas_call | solution.py:527
  34.3 0.7 %copy.6 = f32[32,1024]{1,0:T(8,128)} copy(f32[32,1024]{1,0:T(8,128)S(1)} %shard_map.46) | data formatting | bytes 262144

commit v5 on v4

--- a/solution.py
+++ b/solution.py
@@ -59,13 +59,13 @@
     )
 
 
-def kernel(n, zs, width, basis, blocks, columns, sends, out, *scratch):
+def kernel(n, zs, width, basis, blocks, columns_there, sends_there, out, *scratch):
     chunks = basis.shape[2] // width
     own, scratch = scratch[:chunks], scratch[chunks:]
     ext, scratch = scratch[:chunks], scratch[chunks:]
     (
         stage, relay, turned, ops, diagonal, image, part, pair_out, pair_in, z_out, z_in, x_own, x_out, x_in,
-        far_in, own_sem, ops_sem, halo_send, halo_recv, relay_recv, forward_send,
+        far_in, columns, sends, table_sem, own_sem, ops_sem, halo_send, halo_recv, relay_recv, forward_send,
         pair_send, pair_recv, z_send, z_recv, x_send, x_recv, far_send, far_recv, rounds, go,
     ) = scratch
     params, count, slots, size, _ = blocks.shape
@@ -211,11 +211,17 @@
                 def _():
                     pl.semaphore_signal(sem, inc=1, device_id={"mesh": peer}, device_id_type=MESH)
 
+    sends_copy = pltpu.make_async_copy(sends_there, sends, table_sem.at[0])
+    columns_copy = pltpu.make_async_copy(columns_there, columns, table_sem.at[1])
+    sends_copy.start()
     for k in range(chunks):
         local_copy(k, own, own_sem).start()
     barrier = pltpu.get_barrier_semaphore()
     tell(barrier, close)
+    columns_copy.start()
     ops_copy.start()
+
+    sends_copy.wait()
 
     def direct_start(k, here=True):
         @pl.when(jnp.logical_and(jnp.logical_and(crossing, k < chunks - relayed), here))
@@ -268,13 +274,14 @@
     for k in DIRECT[1]:
         direct_start(k)
     for k in DIRECT[2][:3]:
-        direct_start(k, relayed == 0)
+        direct_start(k, relayed <= (1 - x if k == 1 else 0))
 
     for r in range(zs + 1):
         pl.semaphore_wait(rounds.at[r], close_count if r < CLOSE else near_count)
         if r < zs:
             tell(rounds.at[r + 1], close if r + 1 < CLOSE else near)
 
+    columns_copy.wait()
     ops_copy.wait()
     for k in range(chunks):
         local_copy(k, ext, own_sem).wait()
@@ -290,7 +297,7 @@
     lax.fori_loop(0, count, precompute, 0, unroll=2)
 
     for i, k in enumerate(DIRECT[2]):
-        direct_start(k, relayed > 0 if i < 3 else True)
+        direct_start(k, relayed > (1 - x if k == 1 else 0) if i < 3 else True)
 
     def serve(k):
         if k == last:
@@ -530,8 +537,8 @@
         in_specs=[
             pl.BlockSpec(memory_space=pl.ANY),
             pl.BlockSpec(memory_space=pl.ANY),
-            pl.BlockSpec(memory_space=pltpu.SMEM),
-            pl.BlockSpec(memory_space=pltpu.SMEM),
+            pl.BlockSpec(memory_space=pl.ANY),
+            pl.BlockSpec(memory_space=pl.ANY),
         ],
         out_specs=pl.BlockSpec(memory_space=pltpu.VMEM),
         scratch_shapes=[pltpu.VMEM((count, size, width), bf) for _ in range(chunks)]
@@ -552,6 +559,9 @@
             pltpu.VMEM((hops, tall, wide), bf),
             pltpu.VMEM((hops, 2, each, wide), bf),
             pltpu.VMEM((chunks - hops, n // CORES, each, wide), bf),
+            pltpu.SMEM((params, slots - 1, count), jnp.int32),
+            pltpu.SMEM((1, 2 * halo), jnp.int32),
+            dma((2,)),
             dma((chunks,)),
             dma,
             dma((3,)),

time: 35.1 us -> 34.4 us (0.980)
  Pallas kernels: 34.3 us -> 33.6 us
    pallas_call x1, Pallas kernels: 34.3 us -> 33.6 us  [fused_shards(): pl.pallas_call(functools.partial(kernel, n, zs, width), out_shape=pltpu.V...]
where the time goes in v5:
time: 34.4 us; the launch traced here: 34.3 us
  Pallas kernels  33.6 us (98%)
  local copies, waits for them, and re-layouts  0.66 us (2%)
    pallas_call x1, Pallas kernels, fused_shards(): pl.pallas_call(functools.partial(kernel, n, zs, width), out_shape=pltpu.V...  33.6 us

profile of v5, /device:TPU:0, one launch (start us, length us, event | category | flops | bytes accessed | tf_op | source)
XLA Modules:
  0.0 34.3 jit_solution(18172629140899177177)
XLA Ops:
  0.0 33.6 %shard_map.46 = f32[32,1024]{1,0:T(8,128)S(1)} custom-call(bf16[16,128,512]{2,1,0:T(8,128)(2,1)} %bitcast.2, bf16[2,16,3,128,128]{4,3,2,1,0:T(8,128)(2,1)} %blocks.1, s32[2,2,16]{2,1,0:T(2,128)} %bitcast.3, s32[1,16]{1,0:T(1,128)} %sends_there.1), custom_call_target="tpu_custom_call" | custom-call | tf_op jit(solution)/shard_map/pallas_call | solution.py:534
  33.6 0.7 %copy.6 = f32[32,1024]{1,0:T(8,128)} copy(f32[32,1024]{1,0:T(8,128)S(1)} %shard_map.46) | data formatting | bytes 262144
